TPU v7x, 256 devices: a whole 4x4x8 slice. The times are simulated.
256 devices in a mesh: rad: 32 (over x, y, core), pol: 8 (over z).
Axes of the slice: x: 4, y: 4, z: 8, core: 2. Of those that a mesh axis runs over, the one named last changes fastest.
Arguments:
- dust: float32 [128, 64, 16384], P(None, 'pol', 'rad'), may hold values from 0.2 to 2
- drift_courant: float32 [128], replicated, may hold values from 0.1 to 0.6
- mixing: float32 [128], replicated, may hold values from 0.02 to 0.1
- pair_table: int32 [3, 2048], replicated, may hold values from 0 to 127
- pair_rate: float32 [2048], replicated, may hold values from 0.002 to 0.02
- absorption: float32 [128, 128], replicated, may hold values from 0.05 to 5
- stellar_flux: float32 [128], replicated, may hold values from 0.01 to 0.1
- band_channel: int32 [128], replicated, may hold values from 0 to 3
Outputs:
- new_dust: float32 [128, 64, 16384], P(None, 'pol', 'rad')
- heating: float32 [4, 64, 16384], P(None, 'pol', 'rad')
Inputs may be any that keep to these rules, and one draw needn't show every extreme that they name: `pair_table`: sizes of dust.
All inputs are finite; a program needn't handle non-finite values.
Results may differ from a plain program's by a relative error of at most 0.00005.
Values sent between devices are 32-bit elements; how exact they have to be, the bound alone decides.
A program may use at most 192 MiB of HBM per device.

v0:
```python
import jax
import jax.numpy as jnp
from jax import lax
from jax.sharding import PartitionSpec as P

CH = 4


depth_scale = 4.0


def padded_2(cells, sides, width):
    for axis, dim in sides:
        count = lax.axis_size(axis)
        ends = count - 1
        head = lax.slice_in_dim(cells, 0, width, axis=dim)
        tail = lax.slice_in_dim(cells, cells.shape[dim] - width, cells.shape[dim], axis=dim)
        cells = jnp.concatenate(
            [
                lax.ppermute(tail, axis, [(i, (i + 1) % count) for i in range(ends)]),
                cells,
                lax.ppermute(head, axis, [((i + 1) % count, i) for i in range(ends)]),
            ],
            axis=dim,
        )
    return cells


def collide(advected, pair_table, pair_rate):
    sizes = advected.shape[0]
    grid = jnp.arange(sizes, dtype=jnp.int32)
    first = pair_table[0]
    second = pair_table[1]
    target = pair_table[2]
    pick_first = (first[:, None] == grid[None, :]).astype(jnp.float32)
    pick_second = (second[:, None] == grid[None, :]).astype(jnp.float32)
    redistribute = (grid[:, None] == target[None, :]).astype(jnp.float32)
    redistribute = redistribute - (grid[:, None] == first[None, :]).astype(jnp.float32)
    redistribute = redistribute - (grid[:, None] == second[None, :]).astype(jnp.float32)

    def one_row(column):
        left_part = jnp.dot(
            pick_first, column, precision=lax.Precision.HIGHEST, preferred_element_type=jnp.float32
        )
        right_part = jnp.dot(
            pick_second, column, precision=lax.Precision.HIGHEST, preferred_element_type=jnp.float32
        )
        product = pair_rate[:, None] * left_part * right_part
        return column + jnp.dot(
            redistribute,
            product,
            precision=lax.Precision.HIGHEST,
            preferred_element_type=jnp.float32,
        )

    rows = lax.map(one_row, jnp.moveaxis(advected, 1, 0))
    return jnp.moveaxis(rows, 0, 1)


def shards(
    dust, drift_courant, mixing, pair_table, pair_rate, absorption, stellar_flux, band_channel
):
    padded = padded_2(dust, (("rad", 2), ("pol", 1)), 1)
    center = padded[:, 1:-1, 1:-1]
    outer = padded[:, 1:-1, 2:]
    inner = padded[:, 1:-1, :-2]
    upper = padded[:, 2:, 1:-1]
    lower = padded[:, :-2, 1:-1]
    drift = drift_courant[:, None, None]
    spread = mixing[:, None, None]
    advected = (
        center + drift * (outer - center) + spread * (outer + inner + upper + lower - 4.0 * center)
    )
    new_dust = collide(advected, pair_table, pair_rate)
    sizes = absorption.shape[1]
    opacity = (
        jnp.einsum("bs,str->btr", absorption, new_dust, precision=lax.Precision.HIGHEST) / sizes
    )
    tile = dust.shape[2]
    rad_count = lax.axis_size("rad")
    ray_length = tile * rad_count
    cell_index = jnp.arange(tile, dtype=jnp.int32)
    strict_upper = (cell_index[:, None] < cell_index[None, :]).astype(jnp.float32)
    channels = jnp.arange(CH, dtype=jnp.int32)
    ray_block = lax.all_to_all(opacity, "rad", split_axis=0, concat_axis=2, tiled=True)
    local_bands = ray_block.shape[0]
    polar_rows = ray_block.shape[1]
    first_band = lax.axis_index("rad") * local_bands
    step_depth = ray_block * (depth_scale / ray_length)
    pieces = step_depth.reshape(local_bands, polar_rows, rad_count, tile)
    within = jnp.einsum("bkni,ij->bknj", pieces, strict_upper, precision=lax.Precision.HIGHEST)
    totals = jnp.sum(pieces, axis=3)
    offsets = jnp.cumsum(totals, axis=2) - totals
    depth = (within + offsets[..., None]).reshape(step_depth.shape)
    flux_part = lax.dynamic_slice_in_dim(stellar_flux, first_band, local_bands)
    channel_part = lax.dynamic_slice_in_dim(band_channel, first_band, local_bands)
    absorbed = flux_part[:, None, None] * jnp.exp(-depth) * -jnp.expm1(-step_depth) * ray_length
    picker = (channels[:, None] == channel_part[None, :]).astype(jnp.float32)
    partial_heat = jnp.einsum("cb,bkr->ckr", picker, absorbed, precision=lax.Precision.HIGHEST)
    heating = lax.psum_scatter(partial_heat, "rad", scatter_dimension=2, tiled=True)
    return (new_dust, heating)


def solution(mesh):
    placed = (P(None, "pol", "rad"), P(), P(), P(), P(), P(), P(), P())
    return jax.shard_map(
        shards,
        mesh=mesh,
        in_specs=placed,
        out_specs=(P(None, "pol", "rad"), P(None, "pol", "rad")),
        check_vma=False,
    )
```

profile of v0, /device:TPU:1, one launch (start us, length us, event | category | flops | bytes accessed | tf_op | source)
XLA Modules:
  0.0 392.3 jit_solution(9531429614701989408)
XLA Ops:
  7.2 0.0 copy-start
  7.2 2.0 copy.58
  9.2 0.0 copy-start.4
  9.2 0.0 copy-start.5
  9.2 0.0 copy-start.6
  9.3 4.6 %collective-permute-start.1 = (f32[128,8,1]{0,2,1:T(1,128)S(1)}, f32[128,8,1]{0,2,1:T(1,128)S(1)}, u32[]{:S(2)}, u32[]{:S(2)}) collective-permute-start(f32[128,8,1]{0,2,1:T(1,128)S(1)} %get-tuple-element.115), channel_id=1, source_target_pairs={{0,8},{8,16},{16,24},{24,32},{32,40},{40,48},{48,56},{56,64},{64,7... | collective-permute-start | bytes 12296 | tf_op jit(solution)/shard_map/ppermute | solution.py:20
  13.8 1.9 collective-permute-start
  15.8 0.0 collective-permute-done.1
  15.8 3.0 collective-permute-done
  18.8 1.3 collective-permute-start.2
  20.1 4.2 %collective-permute-start.3 = (f32[128,1,514]{0,2,1:T(8,128)S(1)}, f32[128,1,514]{0,2,1:T(8,128)S(1)}, u32[]{:S(2)}, u32[]{:S(2)}) collective-permute-start(f32[128,1,514]{0,2,1:T(8,128)S(1)} %get-tuple-element.112), channel_id=1, source_target_pairs={{0,1},{1,2},{2,3},{3,4},{4,5},{5,6},{6,7},{8,9},{9,10},{10,11},{11... | collective-permute-start | bytes 789512 | tf_op jit(solution)/shard_map/ppermute | solution.py:20
  24.4 0.0 copy-start.3
  24.4 3.1 collective-permute-done.2
  27.4 1.8 collective-permute-done.3
  29.2 3.2 fusion.46
  32.4 118.0 %while.12 = (s32[]{:T(128)}, f32[8,128,512]{1,2,0:T(8,128)}, f32[8,128,512]{1,2,0:T(8,128)}, f32[2048]{0:T(1024)S(1)}, s32[2048]{0:T(1024)S(1)}, /*index=5*/s32[2048]{0:T(1024)S(1)}, s32[2048]{0:T(1024)S(1)}, s32[]{:T(128)}) while((s32[]{:T(128)}, f32[8,128,512]{1,2,0:T(8,128)}, f32[8,128,512]{1,2,0:T(8,128)}, ...), condition=%wide.region_1.2_spmd.clone.clone, body=%wide.region_0.1_spmd.clone.clone.sunk | while | flops 4837146624 | bytes 17875048 | solution.py:56
  32.4 4.6 %fusion.86 = f32[512,2048]{1,0:T(8,128)S(1)} fusion(s32[2048]{0:T(1024)S(1)} %get-tuple-element.184, f32[8,128,512]{1,2,0:T(8,128)} %get-tuple-element.181, s32[]{:T(128)S(6)} %copy.88), kind=kOutput, calls=%fused_computation.19.clone.1 | convolution fusion | flops 1611137024 | bytes 4464644 | tf_op jit(solution)/shard_map/while/body/eval_jaxpr/dot_general | solution.py:45
  37.0 4.6 %fusion.87 = f32[512,2048]{1,0:T(8,128)S(1)} fusion(s32[2048]{0:T(1024)S(1)} %get-tuple-element.183, f32[8,128,512]{1,2,0:T(8,128)} %get-tuple-element.181, s32[]{:T(128)S(6)} %copy.88), kind=kOutput, calls=%fused_computation.22.clone.1 | convolution fusion | flops 1611137024 | bytes 4464644 | tf_op jit(solution)/shard_map/while/body/eval_jaxpr/dot_general | solution.py:42
  41.6 5.6 %fusion.88 = f32[8,128,512]{1,2,0:T(8,128)} fusion(f32[8,128,512]{1,2,0:T(8,128)} %get-tuple-element.172, s32[]{:T(128)S(6)} %copy.88, f32[512,2048]{1,0:T(8,128)S(1)} %fusion.86, f32[512,2048]{1,0:T(8,128)S(1)} %fusion.87, f32[2048]{0:T(1024)S(1)} %get-tuple-element.182, s32[2048]{0:T(1024)S(1)} %get-tuple-element.184, ...), kind=kOutput, calls=%fused_computation.10.clone.1 | convolution fusion | flops 1614872576 | bytes 8945668 | tf_op jit(solution)/shard_map/while/body/eval_jaxpr/dot_general | solution.py:49
  47.1 4.6 %fusion.86 = f32[512,2048]{1,0:T(8,128)S(1)} fusion(s32[2048]{0:T(1024)S(1)} %get-tuple-element.184, f32[8,128,512]{1,2,0:T(8,128)} %get-tuple-element.181, s32[]{:T(128)S(6)} %copy.88), kind=kOutput, calls=%fused_computation.19.clone.1 | convolution fusion | flops 1611137024 | bytes 4464644 | tf_op jit(solution)/shard_map/while/body/eval_jaxpr/dot_general | solution.py:45
  51.7 4.6 %fusion.87 = f32[512,2048]{1,0:T(8,128)S(1)} fusion(s32[2048]{0:T(1024)S(1)} %get-tuple-element.183, f32[8,128,512]{1,2,0:T(8,128)} %get-tuple-element.181, s32[]{:T(128)S(6)} %copy.88), kind=kOutput, calls=%fused_computation.22.clone.1 | convolution fusion | flops 1611137024 | bytes 4464644 | tf_op jit(solution)/shard_map/while/body/eval_jaxpr/dot_general | solution.py:42
  56.3 5.6 %fusion.88 = f32[8,128,512]{1,2,0:T(8,128)} fusion(f32[8,128,512]{1,2,0:T(8,128)} %get-tuple-element.172, s32[]{:T(128)S(6)} %copy.88, f32[512,2048]{1,0:T(8,128)S(1)} %fusion.86, f32[512,2048]{1,0:T(8,128)S(1)} %fusion.87, f32[2048]{0:T(1024)S(1)} %get-tuple-element.182, s32[2048]{0:T(1024)S(1)} %get-tuple-element.184, ...), kind=kOutput, calls=%fused_computation.10.clone.1 | convolution fusion | flops 1614872576 | bytes 8945668 | tf_op jit(solution)/shard_map/while/body/eval_jaxpr/dot_general | solution.py:49
  61.9 4.6 %fusion.86 = f32[512,2048]{1,0:T(8,128)S(1)} fusion(s32[2048]{0:T(1024)S(1)} %get-tuple-element.184, f32[8,128,512]{1,2,0:T(8,128)} %get-tuple-element.181, s32[]{:T(128)S(6)} %copy.88), kind=kOutput, calls=%fused_computation.19.clone.1 | convolution fusion | flops 1611137024 | bytes 4464644 | tf_op jit(solution)/shard_map/while/body/eval_jaxpr/dot_general | solution.py:45
  66.5 4.6 %fusion.87 = f32[512,2048]{1,0:T(8,128)S(1)} fusion(s32[2048]{0:T(1024)S(1)} %get-tuple-element.183, f32[8,128,512]{1,2,0:T(8,128)} %get-tuple-element.181, s32[]{:T(128)S(6)} %copy.88), kind=kOutput, calls=%fused_computation.22.clone.1 | convolution fusion | flops 1611137024 | bytes 4464644 | tf_op jit(solution)/shard_map/while/body/eval_jaxpr/dot_general | solution.py:42
  71.1 5.6 %fusion.88 = f32[8,128,512]{1,2,0:T(8,128)} fusion(f32[8,128,512]{1,2,0:T(8,128)} %get-tuple-element.172, s32[]{:T(128)S(6)} %copy.88, f32[512,2048]{1,0:T(8,128)S(1)} %fusion.86, f32[512,2048]{1,0:T(8,128)S(1)} %fusion.87, f32[2048]{0:T(1024)S(1)} %get-tuple-element.182, s32[2048]{0:T(1024)S(1)} %get-tuple-element.184, ...), kind=kOutput, calls=%fused_computation.10.clone.1 | convolution fusion | flops 1614872576 | bytes 8945668 | tf_op jit(solution)/shard_map/while/body/eval_jaxpr/dot_general | solution.py:49
  76.6 4.6 %fusion.86 = f32[512,2048]{1,0:T(8,128)S(1)} fusion(s32[2048]{0:T(1024)S(1)} %get-tuple-element.184, f32[8,128,512]{1,2,0:T(8,128)} %get-tuple-element.181, s32[]{:T(128)S(6)} %copy.88), kind=kOutput, calls=%fused_computation.19.clone.1 | convolution fusion | flops 1611137024 | bytes 4464644 | tf_op jit(solution)/shard_map/while/body/eval_jaxpr/dot_general | solution.py:45
  81.2 4.6 %fusion.87 = f32[512,2048]{1,0:T(8,128)S(1)} fusion(s32[2048]{0:T(1024)S(1)} %get-tuple-element.183, f32[8,128,512]{1,2,0:T(8,128)} %get-tuple-element.181, s32[]{:T(128)S(6)} %copy.88), kind=kOutput, calls=%fused_computation.22.clone.1 | convolution fusion | flops 1611137024 | bytes 4464644 | tf_op jit(solution)/shard_map/while/body/eval_jaxpr/dot_general | solution.py:42
  85.8 5.6 %fusion.88 = f32[8,128,512]{1,2,0:T(8,128)} fusion(f32[8,128,512]{1,2,0:T(8,128)} %get-tuple-element.172, s32[]{:T(128)S(6)} %copy.88, f32[512,2048]{1,0:T(8,128)S(1)} %fusion.86, f32[512,2048]{1,0:T(8,128)S(1)} %fusion.87, f32[2048]{0:T(1024)S(1)} %get-tuple-element.182, s32[2048]{0:T(1024)S(1)} %get-tuple-element.184, ...), kind=kOutput, calls=%fused_computation.10.clone.1 | convolution fusion | flops 1614872576 | bytes 8945668 | tf_op jit(solution)/shard_map/while/body/eval_jaxpr/dot_general | solution.py:49
  91.4 4.6 %fusion.86 = f32[512,2048]{1,0:T(8,128)S(1)} fusion(s32[2048]{0:T(1024)S(1)} %get-tuple-element.184, f32[8,128,512]{1,2,0:T(8,128)} %get-tuple-element.181, s32[]{:T(128)S(6)} %copy.88), kind=kOutput, calls=%fused_computation.19.clone.1 | convolution fusion | flops 1611137024 | bytes 4464644 | tf_op jit(solution)/shard_map/while/body/eval_jaxpr/dot_general | solution.py:45
  96.0 4.6 %fusion.87 = f32[512,2048]{1,0:T(8,128)S(1)} fusion(s32[2048]{0:T(1024)S(1)} %get-tuple-element.183, f32[8,128,512]{1,2,0:T(8,128)} %get-tuple-element.181, s32[]{:T(128)S(6)} %copy.88), kind=kOutput, calls=%fused_computation.22.clone.1 | convolution fusion | flops 1611137024 | bytes 4464644 | tf_op jit(solution)/shard_map/while/body/eval_jaxpr/dot_general | solution.py:42
  100.6 5.6 %fusion.88 = f32[8,128,512]{1,2,0:T(8,128)} fusion(f32[8,128,512]{1,2,0:T(8,128)} %get-tuple-element.172, s32[]{:T(128)S(6)} %copy.88, f32[512,2048]{1,0:T(8,128)S(1)} %fusion.86, f32[512,2048]{1,0:T(8,128)S(1)} %fusion.87, f32[2048]{0:T(1024)S(1)} %get-tuple-element.182, s32[2048]{0:T(1024)S(1)} %get-tuple-element.184, ...), kind=kOutput, calls=%fused_computation.10.clone.1 | convolution fusion | flops 1614872576 | bytes 8945668 | tf_op jit(solution)/shard_map/while/body/eval_jaxpr/dot_general | solution.py:49
  106.1 4.6 %fusion.86 = f32[512,2048]{1,0:T(8,128)S(1)} fusion(s32[2048]{0:T(1024)S(1)} %get-tuple-element.184, f32[8,128,512]{1,2,0:T(8,128)} %get-tuple-element.181, s32[]{:T(128)S(6)} %copy.88), kind=kOutput, calls=%fused_computation.19.clone.1 | convolution fusion | flops 1611137024 | bytes 4464644 | tf_op jit(solution)/shard_map/while/body/eval_jaxpr/dot_general | solution.py:45
  110.7 4.6 %fusion.87 = f32[512,2048]{1,0:T(8,128)S(1)} fusion(s32[2048]{0:T(1024)S(1)} %get-tuple-element.183, f32[8,128,512]{1,2,0:T(8,128)} %get-tuple-element.181, s32[]{:T(128)S(6)} %copy.88), kind=kOutput, calls=%fused_computation.22.clone.1 | convolution fusion | flops 1611137024 | bytes 4464644 | tf_op jit(solution)/shard_map/while/body/eval_jaxpr/dot_general | solution.py:42
  115.3 5.6 %fusion.88 = f32[8,128,512]{1,2,0:T(8,128)} fusion(f32[8,128,512]{1,2,0:T(8,128)} %get-tuple-element.172, s32[]{:T(128)S(6)} %copy.88, f32[512,2048]{1,0:T(8,128)S(1)} %fusion.86, f32[512,2048]{1,0:T(8,128)S(1)} %fusion.87, f32[2048]{0:T(1024)S(1)} %get-tuple-element.182, s32[2048]{0:T(1024)S(1)} %get-tuple-element.184, ...), kind=kOutput, calls=%fused_computation.10.clone.1 | convolution fusion | flops 1614872576 | bytes 8945668 | tf_op jit(solution)/shard_map/while/body/eval_jaxpr/dot_general | solution.py:49
  120.9 4.6 %fusion.86 = f32[512,2048]{1,0:T(8,128)S(1)} fusion(s32[2048]{0:T(1024)S(1)} %get-tuple-element.184, f32[8,128,512]{1,2,0:T(8,128)} %get-tuple-element.181, s32[]{:T(128)S(6)} %copy.88), kind=kOutput, calls=%fused_computation.19.clone.1 | convolution fusion | flops 1611137024 | bytes 4464644 | tf_op jit(solution)/shard_map/while/body/eval_jaxpr/dot_general | solution.py:45
  125.5 4.6 %fusion.87 = f32[512,2048]{1,0:T(8,128)S(1)} fusion(s32[2048]{0:T(1024)S(1)} %get-tuple-element.183, f32[8,128,512]{1,2,0:T(8,128)} %get-tuple-element.181, s32[]{:T(128)S(6)} %copy.88), kind=kOutput, calls=%fused_computation.22.clone.1 | convolution fusion | flops 1611137024 | bytes 4464644 | tf_op jit(solution)/shard_map/while/body/eval_jaxpr/dot_general | solution.py:42
  130.1 5.6 %fusion.88 = f32[8,128,512]{1,2,0:T(8,128)} fusion(f32[8,128,512]{1,2,0:T(8,128)} %get-tuple-element.172, s32[]{:T(128)S(6)} %copy.88, f32[512,2048]{1,0:T(8,128)S(1)} %fusion.86, f32[512,2048]{1,0:T(8,128)S(1)} %fusion.87, f32[2048]{0:T(1024)S(1)} %get-tuple-element.182, s32[2048]{0:T(1024)S(1)} %get-tuple-element.184, ...), kind=kOutput, calls=%fused_computation.10.clone.1 | convolution fusion | flops 1614872576 | bytes 8945668 | tf_op jit(solution)/shard_map/while/body/eval_jaxpr/dot_general | solution.py:49
  135.6 4.6 %fusion.86 = f32[512,2048]{1,0:T(8,128)S(1)} fusion(s32[2048]{0:T(1024)S(1)} %get-tuple-element.184, f32[8,128,512]{1,2,0:T(8,128)} %get-tuple-element.181, s32[]{:T(128)S(6)} %copy.88), kind=kOutput, calls=%fused_computation.19.clone.1 | convolution fusion | flops 1611137024 | bytes 4464644 | tf_op jit(solution)/shard_map/while/body/eval_jaxpr/dot_general | solution.py:45
  140.2 4.6 %fusion.87 = f32[512,2048]{1,0:T(8,128)S(1)} fusion(s32[2048]{0:T(1024)S(1)} %get-tuple-element.183, f32[8,128,512]{1,2,0:T(8,128)} %get-tuple-element.181, s32[]{:T(128)S(6)} %copy.88), kind=kOutput, calls=%fused_computation.22.clone.1 | convolution fusion | flops 1611137024 | bytes 4464644 | tf_op jit(solution)/shard_map/while/body/eval_jaxpr/dot_general | solution.py:42
  144.8 5.6 %fusion.88 = f32[8,128,512]{1,2,0:T(8,128)} fusion(f32[8,128,512]{1,2,0:T(8,128)} %get-tuple-element.172, s32[]{:T(128)S(6)} %copy.88, f32[512,2048]{1,0:T(8,128)S(1)} %fusion.86, f32[512,2048]{1,0:T(8,128)S(1)} %fusion.87, f32[2048]{0:T(1024)S(1)} %get-tuple-element.182, s32[2048]{0:T(1024)S(1)} %get-tuple-element.184, ...), kind=kOutput, calls=%fused_computation.10.clone.1 | convolution fusion | flops 1614872576 | bytes 8945668 | tf_op jit(solution)/shard_map/while/body/eval_jaxpr/dot_general | solution.py:49
  150.4 3.4 multiply_bitcast_fusion
  153.8 2.0 copy.65
  155.8 8.1 %all-to-all-start = ((f32[128,8,512]{2,1,0:T(8,128)}), f32[128,8,512]{2,1,0:T(8,128)}, u32[]{:S(2)}, u32[]{:S(2)}) async-start(f32[128,8,512]{2,1,0:T(8,128)} %copy.65), calls=%async_computation | async-start | bytes 4194304 | tf_op jit(solution)/shard_map/all_to_all | solution.py:85
  163.9 0.0 reduce-scatter.4.cloned.1.call-start
  164.0 0.1 dynamic_slice.11
  164.1 0.0 copy-done.8
  164.1 0.1 dynamic_slice.10
  164.1 28.2 %all-to-all-done = f32[128,8,512]{2,1,0:T(8,128)} async-done(((f32[128,8,512]{2,1,0:T(8,128)}), f32[128,8,512]{2,1,0:T(8,128)}, u32[]{:S(2)}, u32[]{:S(2)}) %all-to-all-start) | async-done | bytes 2097184 | tf_op jit(solution)/shard_map/all_to_all | solution.py:85
  192.3 2.3 broadcast_multiply_fusion
  194.7 1.5 copy.75
  196.2 1.2 bitcast_reduce_fusion
  197.3 0.7 reduce_window_sum.11
  198.1 4.2 %negate_exponential_fusion = f32[4,8,32,512]{3,2,1,0:T(8,128)} fusion(f32[32,4,8,512]{3,2,1,0:T(8,128)S(1)} %bitcast.70, f32[4,8,32]{2,1,0:T(8,128)S(1)} %sub.23), kind=kOutput, calls=%fused_computation.63 | convolution fusion | flops 3222536192 | bytes 4198400 | tf_op jit(solution)/shard_map/bkni,ij->bknj/dot_general | solution.py:91
  202.3 2.9 exp.7
  205.2 1.9 multiply_multiply_fusion
  207.1 3.2 fusion.56
  210.3 30.8 %copy.72 = f32[4,8,16384]{0,1,2:T(8,128)} copy(f32[4,8,16384]{2,0,1:T(4,128)S(1)} %fusion.56) | data formatting | bytes 4194304
  241.1 41.7 %reshape.39 = f32[16384,32]{1,0:T(8,128)} reshape(f32[16384,8,4]{2,1,0:T(8,128)} %bitcast.19) | data formatting | bytes 4194304
  282.8 0.0 reduce-scatter.4.cloned.1.call-update
  282.8 1.6 copy-done.2
  284.4 2.0 copy.63
  286.4 96.1 %reduce-scatter.4.cloned.1.call-done = f32[512,32]{1,0:T(8,128)} async-done(((f32[16384,32]{1,0:T(8,128)}), f32[512,32]{1,0:T(8,128)}) %reduce-scatter.4.cloned.1.call-update) | async-done | bytes 65552
  382.4 1.6 reshape.40
  384.1 1.4 copy.69
  (16 shorter events, 0.1 us)
Async XLA Ops:
  7.2 143.2 %copy-start = (f32[128,128]{1,0:T(8,128)S(1)}, f32[128,128]{1,0:T(8,128)}, u32[]{:S(2)}) copy-start(f32[128,128]{1,0:T(8,128)} %param.15) | copy-start | bytes 196612
  9.2 15.1 %copy-start.4 = (s32[3,2048]{1,0:T(4,128)S(1)}, s32[3,2048]{1,0:T(4,128)}, u32[]{:S(2)}) copy-start(s32[3,2048]{1,0:T(4,128)} %param.13) | copy-start | bytes 73732
  9.2 20.0 %copy-start.5 = (f32[128]{0:T(128)S(1)}, f32[128]{0:T(128)}, u32[]{:S(2)}) copy-start(f32[128]{0:T(128)} %param.12) | copy-start | bytes 1540
  9.2 20.0 %copy-start.6 = (f32[128]{0:T(128)S(1)}, f32[128]{0:T(128)}, u32[]{:S(2)}) copy-start(f32[128]{0:T(128)} %param.11) | copy-start | bytes 1540
  9.3 6.5 %collective-permute-start.1 = (f32[128,8,1]{0,2,1:T(1,128)S(1)}, f32[128,8,1]{0,2,1:T(1,128)S(1)}, u32[]{:S(2)}, u32[]{:S(2)}) collective-permute-start(f32[128,8,1]{0,2,1:T(1,128)S(1)} %get-tuple-element.115), channel_id=1, source_target_pairs={{0,8},{8,16},{16,24},{24,32},{32,40},{40,48},{48,56},{56,64},{64,7... | collective-permute-start | bytes 12296 | tf_op jit(solution)/shard_map/ppermute | solution.py:20
  13.8 4.9 %collective-permute-start = (f32[128,8,1]{0,2,1:T(1,128)S(1)}, f32[128,8,1]{0,2,1:T(1,128)S(1)}, u32[]{:S(2)}, u32[]{:S(2)}) collective-permute-start(f32[128,8,1]{0,2,1:T(1,128)S(1)} %get-tuple-element.116), channel_id=1, source_target_pairs={{8,0},{16,8},{24,16},{32,24},{40,32},{48,40},{56,48},{64,56},{72,6... | collective-permute-start | bytes 12296 | tf_op jit(solution)/shard_map/ppermute | solution.py:22
  18.8 8.6 %collective-permute-start.2 = (f32[128,1,514]{0,2,1:T(8,128)S(1)}, f32[128,1,514]{0,2,1:T(8,128)S(1)}, u32[]{:S(2)}, u32[]{:S(2)}) collective-permute-start(f32[128,1,514]{0,2,1:T(8,128)S(1)} %get-tuple-element.111), channel_id=1, source_target_pairs={{1,0},{2,1},{3,2},{4,3},{5,4},{6,5},{7,6},{9,8},{10,9},{11,10},{12... | collective-permute-start | bytes 789512 | tf_op jit(solution)/shard_map/ppermute | solution.py:22
  20.1 9.1 %collective-permute-start.3 = (f32[128,1,514]{0,2,1:T(8,128)S(1)}, f32[128,1,514]{0,2,1:T(8,128)S(1)}, u32[]{:S(2)}, u32[]{:S(2)}) collective-permute-start(f32[128,1,514]{0,2,1:T(8,128)S(1)} %get-tuple-element.112), channel_id=1, source_target_pairs={{0,1},{1,2},{2,3},{3,4},{4,5},{5,6},{6,7},{8,9},{9,10},{10,11},{11... | collective-permute-start | bytes 789512 | tf_op jit(solution)/shard_map/ppermute | solution.py:20
  24.4 8.0 %copy-start.3 = (f32[2048]{0:T(1024)S(1)}, f32[2048]{0:T(1024)}, u32[]{:S(2)}) copy-start(f32[2048]{0:T(1024)} %param.14) | copy-start | bytes 24580
  155.8 8.2 %copy-start.7 = (f32[128]{0:T(128)S(1)}, f32[128]{0:T(128)}, u32[]{:S(2)}) copy-start(f32[128]{0:T(128)} %param.16) | copy-start | bytes 1540
  155.8 8.3 %copy-start.8 = (s32[128]{0:T(128)S(1)}, s32[128]{0:T(128)}, u32[]{:S(2)}) copy-start(s32[128]{0:T(128)} %param.17) | copy-start | bytes 1540
  155.8 36.5 %all-to-all-start = ((f32[128,8,512]{2,1,0:T(8,128)}), f32[128,8,512]{2,1,0:T(8,128)}, u32[]{:S(2)}, u32[]{:S(2)}) async-start(f32[128,8,512]{2,1,0:T(8,128)} %copy.65), calls=%async_computation | async-start | bytes 4194304 | tf_op jit(solution)/shard_map/all_to_all | solution.py:85
  163.9 218.5 %reduce-scatter.4.cloned.1.call-start = ((), (), s32[]{:S(2)}) async-start(), calls=%async_computation.2 | async-start | bytes 8650752
  202.3 2.9 copy-start.1
  282.8 1.6 copy-start.2
Sparse Core Ops, SparseCore 0:
  283.0 99.4 reduce-scatter.3
where the time goes:
time: 395 us; the launch traced here: 392 us
  waiting for transfers between devices  132 us (33%)
  matrix products  129 us (33%)
  local copies, waits for them, and re-layouts  87.7 us (22%)
  starting transfers between devices  20.1 us (5%)
  between operations  14.2 us (4%)
  other arithmetic  9.31 us (2%)
    unnamed x2, waiting for transfers between devices  96.1 us
    unnamed x23, local copies, waits for them, and re-layouts  79.1 us
    dot_general x8, matrix products, one_row(): jnp.dot(redistribute, product, precision=lax.Precision.HIGHEST, preferred...  44.4 us
    dot_general x8, matrix products, one_row(): jnp.dot(pick_first, column, precision=lax.Precision.HIGHEST, preferred_el...  36.8 us
    dot_general x8, matrix products, one_row(): jnp.dot(pick_second, column, precision=lax.Precision.HIGHEST, preferred_e...  36.7 us
    all_to_all x1, waiting for transfers between devices, shards(): lax.all_to_all(opacity, 'rad', split_axis=0, concat_axis=2, tiled=True)  28.2 us
    ppermute x2, starting transfers between devices, padded_2(): lax.ppermute(tail, axis, [(i, (i + 1) % count) for i in range(ends)])  8.77 us
    all_to_all x1, starting transfers between devices, shards(): lax.all_to_all(opacity, 'rad', split_axis=0, concat_axis=2, tiled=True)  8.1 us
  transfers between devices with their start and end apart: 6, of which 5 were waited for; matrix products, arithmetic and copies ran while one was open for 1% of the time, Pallas kernels for 0%

commit v1 on v0

v1 whole, which is shorter than its diff:
```python
import functools

import jax
import jax.numpy as jnp
from jax import lax
from jax.experimental import pallas as pl
from jax.experimental.pallas import tpu as pltpu
from jax.sharding import PartitionSpec as P

CH = 4
LANES = 128
SUB = 8
depth_scale = 4.0
SHIFT = 10.0
UNROLL = 16
f32 = jnp.float32
bf16 = jnp.bfloat16


def halves(x):
    hi = x.astype(bf16)
    return hi, (x - hi.astype(f32)).astype(bf16)


def dot_nt(a, b):
    return lax.dot_general(a, b, (((1,), (1,)), ((), ())), preferred_element_type=f32)


def stacked(matrix):
    hi, lo = halves(matrix)
    return jnp.concatenate(
        [jnp.concatenate([hi, hi], axis=1), jnp.concatenate([lo, lo], axis=1)], axis=0
    )


def product(left, right):
    rows = left.shape[0] // 2
    both = jnp.dot(
        left, jnp.concatenate(halves(right), axis=0), preferred_element_type=f32
    )
    return both[:rows] + both[rows:]


def halo_kernel(
    n_rad, n_pol, dust, table, rate, below, above, left, right, rows_at, loss,
    ends, sent, load_sem, send_sem, recv_sem,
):
    sizes = dust.shape[0]
    tile = dust.shape[2]
    rad = lax.axis_index("rad")
    pol = lax.axis_index("pol")
    rad_up, rad_down = lax.rem(rad + 1, n_rad), lax.rem(rad + n_rad - 1, n_rad)
    pol_up, pol_down = lax.rem(pol + 1, n_pol), lax.rem(pol + n_pol - 1, n_pol)
    barrier = pltpu.get_barrier_semaphore()
    pl.semaphore_signal(barrier, inc=1, device_id={"rad": rad_up})
    pl.semaphore_signal(barrier, inc=1, device_id={"rad": rad_down})
    pl.semaphore_signal(barrier, inc=1, device_id={"pol": pol_up})
    pl.semaphore_signal(barrier, inc=1, device_id={"pol": pol_down})
    loads = [
        pltpu.make_async_copy(dust.at[:, :, pl.ds(0, LANES)], ends.at[0], load_sem.at[0]),
        pltpu.make_async_copy(
            dust.at[:, :, pl.ds(tile - LANES, LANES)], ends.at[1], load_sem.at[1]
        ),
    ]
    for load in loads:
        load.start()
    pl.semaphore_wait(barrier, 4)
    copies = [
        pltpu.make_async_remote_copy(
            dust.at[:, SUB - 1, :], below, send_sem.at[0], recv_sem.at[0],
            device_id={"pol": pol_up},
        ),
        pltpu.make_async_remote_copy(
            dust.at[:, 0, :], above, send_sem.at[1], recv_sem.at[1],
            device_id={"pol": pol_down},
        ),
    ]
    for copy in copies:
        copy.start()
    for load in loads:
        load.wait()
    lane = lax.broadcasted_iota(jnp.int32, (SUB, LANES), 1)

    def gather(group, carry):
        first, last = carry
        for step in range(8):
            size = group * 8 + step
            here = lane == size
            first = jnp.where(here, ends[0, size][:, 0:1], first)
            last = jnp.where(here, ends[1, size][:, LANES - 1 :], last)
        return first, last

    zero = jnp.zeros((SUB, LANES), f32)
    first, last = lax.fori_loop(0, sizes // 8, gather, (zero, zero))
    sent[0] = first
    sent[1] = last
    for piece in range(table.shape[1] // LANES):
        for row in range(3):
            rows_at[pl.ds(row * (table.shape[1] // LANES) + piece, 1), :] = (
                table[row : row + 1, LANES * piece : LANES * piece + LANES] * (4 * SUB)
            )
    edges = [
        pltpu.make_async_remote_copy(
            sent.at[1], left, send_sem.at[2], recv_sem.at[2], device_id={"rad": rad_up}
        ),
        pltpu.make_async_remote_copy(
            sent.at[0], right, send_sem.at[3], recv_sem.at[3], device_id={"rad": rad_down}
        ),
    ]
    for copy in edges:
        copy.start()

    grid = lax.broadcasted_iota(jnp.int32, (sizes, LANES), 0)
    total = jnp.zeros((sizes, sizes), f32)
    for piece in range(table.shape[1] // LANES):
        cut = slice(LANES * piece, LANES * piece + LANES)
        is_first = grid == table[0:1, cut]
        is_second = grid == table[1:2, cut]
        rates = rate[piece : piece + 1, :]
        ones = jnp.concatenate([is_second, is_first], axis=1).astype(f32).astype(bf16)
        weights = jnp.concatenate(
            [jnp.where(is_first, rates, 0.0), jnp.where(is_second, rates, 0.0)], axis=1
        )
        high, rest = halves(weights)
        total = total + dot_nt(high, ones) + dot_nt(rest, ones)
    loss[...] = total
    for copy in copies + edges:
        copy.wait()


def collide_kernel(
    n_rad, n_pol, dust, below, above, left, right, drift, mixing, rows_at, rate, loss,
    out, adv, gain_a, gain_b,
):
    sizes = dust.shape[0]
    pairs = rate.shape[0]
    pieces = dust.shape[2] // LANES
    span = pieces * SUB
    rad = lax.axis_index("rad")
    pol = lax.axis_index("pol")
    lane = lax.broadcasted_iota(jnp.int32, (SUB, LANES), 1)
    sub = lax.broadcasted_iota(jnp.int32, (SUB, LANES), 0)
    has_left = jnp.where(rad > 0, 1.0, 0.0)
    has_right = jnp.where(rad < n_rad - 1, 1.0, 0.0)
    has_below = jnp.where(pol > 0, 1.0, 0.0)
    has_above = jnp.where(pol < n_pol - 1, 1.0, 0.0)
    zero = jnp.zeros((SUB, LANES), f32)

    def advect(group, carry):
        at_left, at_right = carry
        for step in range(4):
            size = group * 4 + step
            c = drift[size]
            m = mixing[size]
            center = dust[size]
            cells = [center[:, LANES * k : LANES * k + LANES] for k in range(pieces)]
            back = [pltpu.roll(x, LANES - 1, 1) for x in cells] + [at_right]
            forth = [at_left] + [pltpu.roll(x, 1, 1) for x in cells]
            low_row = below[pl.ds(size, 1), :] * has_below
            high_row = above[pl.ds(size, 1), :] * has_above
            for k in range(pieces):
                cut = slice(LANES * k, LANES * k + LANES)
                here = cells[k]
                outer = jnp.where(lane == LANES - 1, back[k + 1], back[k])
                inner = jnp.where(lane == 0, forth[k], forth[k + 1])
                upper = jnp.where(sub == SUB - 1, high_row[:, cut], pltpu.roll(here, SUB - 1, 0))
                lower = jnp.where(sub == 0, low_row[:, cut], pltpu.roll(here, 1, 0))
                value = (
                    here
                    + c * (outer - here)
                    + m * (outer + inner + upper + lower - 4.0 * here)
                )
                rows = pl.ds(pl.multiple_of(size * span + k * SUB, SUB), SUB)
                adv[rows, :] = value
                gain_a[rows, :] = value
                gain_b[rows, :] = zero
            at_left = pltpu.roll(at_left, LANES - 1, 1)
            at_right = pltpu.roll(at_right, LANES - 1, 1)
        return at_left, at_right

    lax.fori_loop(
        0,
        sizes // 4,
        advect,
        (left[...] * has_left, pltpu.roll(right[...] * has_right, LANES - 1, 1)),
    )

    def rows(start):
        return pl.ds(pl.multiple_of(start, span), span)

    def collide(group, _):
        base = group * UNROLL
        for step in range(UNROLL):
            first = rows_at[base + step]
            second = rows_at[base + (pairs + step)]
            target = rows_at[base + (2 * pairs + step)]
            value = (rate[base + step] * adv[rows(first), :]) * adv[rows(second), :]
            gain = gain_a if step % 2 == 0 else gain_b
            gain[rows(target), :] = gain[rows(target), :] + value
        return 0

    lax.fori_loop(0, pairs // UNROLL, collide, 0)

    matrix = stacked(loss[...])
    for t in range(SUB):
        parts = [pl.ds(k * SUB + t, sizes, stride=span) for k in range(pieces)]
        here = jnp.concatenate([adv[part, :] for part in parts], axis=1)
        lost = here * product(matrix, here)
        for k in range(pieces):
            cut = slice(LANES * k, LANES * k + LANES)
            out[:, t, cut] = gain_a[parts[k], :] + gain_b[parts[k], :] - lost[:, cut]


def heat_kernel(
    n_rad, dust, absorption, flux, channel, heating,
    steps, factor, tile_total, arrived, send_sem, recv_sem,
):
    sizes = dust.shape[0]
    tile = dust.shape[2]
    bands = absorption.shape[0]
    pieces = tile // LANES
    ray_length = tile * n_rad
    rad = lax.axis_index("rad")
    barrier = pltpu.get_barrier_semaphore()

    def greet(away, _):
        pl.semaphore_signal(barrier, inc=1, device_id={"rad": lax.rem(rad + away, n_rad)})
        return 0

    lax.fori_loop(1, n_rad, greet, 0)

    matrix = stacked(absorption[...] * (depth_scale / (ray_length * sizes)))
    lane = lax.broadcasted_iota(jnp.int32, (bands, LANES), 1)
    column = jnp.zeros((bands, LANES), f32)
    for t in range(SUB):
        step = product(matrix, dust[:, t, :])
        steps[t] = step
        over = step[:, :LANES]
        for k in range(1, pieces):
            over = over + step[:, LANES * k : LANES * k + LANES]
        column = jnp.where(lane == t, jnp.sum(over, axis=1, keepdims=True), column)
    tile_total[...] = jnp.transpose(column)[:SUB]
    pl.semaphore_wait(barrier, n_rad - 1)

    def send(away, _):
        pltpu.make_async_remote_copy(
            tile_total, arrived.at[away - 1], send_sem, recv_sem,
            device_id={"rad": lax.rem(rad + away, n_rad)},
        ).start()
        return 0

    lax.fori_loop(1, n_rad, send, 0)

    row = lax.broadcasted_iota(jnp.int32, (LANES, LANES), 0)
    col = lax.broadcasted_iota(jnp.int32, (LANES, LANES), 1)
    ahead = jnp.concatenate(
        [jnp.where(row < col, 1.0, 0.0), jnp.ones((LANES, LANES), f32)], axis=1
    ).astype(bf16)
    ahead = jnp.concatenate([ahead, ahead], axis=0)
    for t in range(SUB):
        so_far = jnp.zeros((bands, LANES), f32)
        for k in range(pieces):
            cut = slice(LANES * k, LANES * k + LANES)
            x = steps[t, :, cut]
            sums = jnp.dot(
                jnp.concatenate(halves(x), axis=1), ahead, preferred_element_type=f32
            )
            within = so_far + sums[:, :LANES]
            so_far = so_far + sums[:, LANES:]
            series = x * (
                1.0 - x * (0.5 - x * (1.0 / 6 - x * (1.0 / 24 - x * (1.0 / 120 - x * (1.0 / 720)))))
            )
            taken = jnp.where(jnp.abs(x) < 0.1, series, 1.0 - jnp.exp(-x))
            high, low = halves(jnp.exp(SHIFT - within) * taken * ray_length)
            factor[t, 0:bands, cut] = high
            factor[t, bands : 2 * bands, cut] = low

    pltpu.make_async_copy(arrived, arrived, recv_sem).wait()
    offset = jnp.zeros((SUB, bands), f32)
    for away in range(1, n_rad):
        offset = offset + jnp.where(rad >= away, arrived[away - 1], 0.0)
    weight = flux[...] * jnp.exp(-offset - SHIFT)
    which = lax.broadcasted_iota(jnp.int32, (SUB, bands), 0) == channel[...]
    for t in range(SUB):
        high, low = halves(jnp.where(which, weight[t : t + 1, :], 0.0))
        left = jnp.concatenate(
            [jnp.concatenate([high, high], axis=1), jnp.concatenate([low, low], axis=1)], axis=0
        )
        both = jnp.dot(left, factor[t], preferred_element_type=f32)
        heating[:, t, :] = (both[:SUB] + both[SUB:])[:CH]
    pltpu.make_async_copy(arrived, arrived, send_sem).wait()


VMEM = pl.BlockSpec(memory_space=pltpu.VMEM)
SMEM = pl.BlockSpec(memory_space=pltpu.SMEM)
ANY = pl.BlockSpec(memory_space=pl.ANY)


def shards(
    dust, drift_courant, mixing, pair_table, pair_rate, absorption, stellar_flux, band_channel
):
    n_rad = lax.axis_size("rad")
    n_pol = lax.axis_size("pol")
    sizes, rows, tile = dust.shape
    pairs = pair_rate.shape[0]
    bands = absorption.shape[0]
    pieces = tile // LANES

    def like(*shape, dtype=f32):
        return jax.ShapeDtypeStruct(shape, dtype)

    below, above, left, right, rows_at, loss = pl.pallas_call(
        functools.partial(halo_kernel, n_rad, n_pol),
        out_shape=(
            like(sizes, tile),
            like(sizes, tile),
            like(rows, sizes),
            like(rows, sizes),
            like(3 * pairs // LANES, LANES, dtype=jnp.int32),
            like(sizes, sizes),
        ),
        in_specs=[ANY, VMEM, VMEM],
        out_specs=(VMEM,) * 6,
        scratch_shapes=[
            pltpu.VMEM((2, sizes, rows, LANES), f32),
            pltpu.VMEM((2, rows, sizes), f32),
            pltpu.SemaphoreType.DMA((2,)),
            pltpu.SemaphoreType.DMA((4,)),
            pltpu.SemaphoreType.DMA((4,)),
        ],
        compiler_params=pltpu.CompilerParams(collective_id=0, has_side_effects=True),
        name="halo",
    )(dust, pair_table, pair_rate.reshape(pairs // LANES, LANES))
    new_dust = pl.pallas_call(
        functools.partial(collide_kernel, n_rad, n_pol),
        out_shape=like(sizes, rows, tile),
        in_specs=[VMEM] * 5 + [SMEM] * 4 + [VMEM],
        out_specs=VMEM,
        scratch_shapes=[pltpu.VMEM((sizes * pieces * SUB, LANES), f32)] * 3,
        name="collide",
    )(
        dust, below, above, left, right, drift_courant, mixing,
        rows_at.reshape(3 * pairs), pair_rate, loss,
    )
    heating = pl.pallas_call(
        functools.partial(heat_kernel, n_rad),
        out_shape=like(CH, rows, tile),
        in_specs=[VMEM] * 4,
        out_specs=VMEM,
        scratch_shapes=[
            pltpu.VMEM((rows, bands, tile), f32),
            pltpu.VMEM((rows, 2 * bands, tile), bf16),
            pltpu.VMEM((rows, bands), f32),
            pltpu.VMEM((n_rad - 1, rows, bands), f32),
            pltpu.SemaphoreType.DMA,
            pltpu.SemaphoreType.DMA,
        ],
        compiler_params=pltpu.CompilerParams(collective_id=1, has_side_effects=True),
        name="heat",
    )(new_dust, absorption, stellar_flux.reshape(1, bands), band_channel.reshape(1, bands))
    return new_dust, heating


def solution(mesh):
    placed = (P(None, "pol", "rad"), P(), P(), P(), P(), P(), P(), P())
    return jax.shard_map(
        shards,
        mesh=mesh,
        in_specs=placed,
        out_specs=(P(None, "pol", "rad"), P(None, "pol", "rad")),
        check_vma=False,
    )
```

time: 395 us -> 60.2 us (0.15)
  waiting for transfers between devices: 132 us -> 0 us
  matrix products: 129 us -> 0 us
  local copies, waits for them, and re-layouts: 87.7 us -> 1.47 us
  Pallas kernels: 0 us -> 57.8 us
  starting transfers between devices: 20.1 us -> 0 us
  between operations: 14.2 us -> 0.65 us
  other arithmetic: 9.31 us -> 0 us
    dot_general x27 -> x0, matrix products: 129 us -> none  [the longest x8 44.4 us: one_row(): jnp.dot(redistribute, product, precision=lax.Precision.HIGHEST, preferred...]
    unnamed x2 -> x0, waiting for transfers between devices: 96.1 us -> none
    unnamed x23 -> x1, local copies, waits for them, and re-layouts: 79.1 us -> 1.47 us
    pallas_call x0 -> x3, Pallas kernels: none -> 57.8 us  [the longest x1 23.5 us: shards(): pl.pallas_call(functools.partial(collide_kernel, n_rad, n_pol), out_shape...]
    all_to_all x1 -> x0, waiting for transfers between devices: 28.2 us -> none  [shards(): lax.all_to_all(opacity, 'rad', split_axis=0, concat_axis=2, tiled=True)]
    ppermute x4 -> x0, starting transfers between devices: 12 us -> none  [the longest x2 8.77 us: padded_2(): lax.ppermute(tail, axis, [(i, (i + 1) % count) for i in range(ends)])]
    all_to_all x1 -> x0, starting transfers between devices: 8.1 us -> none  [shards(): lax.all_to_all(opacity, 'rad', split_axis=0, concat_axis=2, tiled=True)]
    ppermute x4 -> x0, waiting for transfers between devices: 7.81 us -> none  [the longest x2 6.05 us: padded_2(): lax.ppermute(head, axis, [((i + 1) % count, i) for i in range(ends)])]
  transfers between devices with their start and end apart: 6 -> 0, of which waited for: 5 -> 0; matrix products, arithmetic and copies ran while one was open for 1% -> 0% of each run, Pallas kernels for 0% -> 0%
where the time goes in v1:
time: 60.2 us; the launch traced here: 59.9 us
  Pallas kernels  57.8 us (96%)
  local copies, waits for them, and re-layouts  1.47 us (2%)
  between operations  0.65 us (1%)
    pallas_call x1, Pallas kernels, shards(): pl.pallas_call(functools.partial(collide_kernel, n_rad, n_pol), out_shape...  23.5 us
    pallas_call x1, Pallas kernels, shards(): pl.pallas_call(functools.partial(heat_kernel, n_rad), out_shape=like(CH,...  20.2 us
    pallas_call x1, Pallas kernels, shards(): pl.pallas_call(functools.partial(halo_kernel, n_rad, n_pol), out_shape=(l...  14 us
    unnamed x1, local copies, waits for them, and re-layouts  1.47 us

profile of v1, /device:TPU:1, one launch (start us, length us, event | category | flops | bytes accessed | tf_op | source)
XLA Modules:
  0.0 59.9 jit_solution(6942142527497995944)
XLA Ops:
  0.6 14.0 %halo.1 = (f32[128,512]{1,0:T(8,128)}, f32[128,512]{1,0:T(8,128)}, f32[8,128]{1,0:T(8,128)}, f32[8,128]{1,0:T(8,128)}, s32[48,128]{1,0:T(8,128)}, /*index=5*/f32[128,128]{1,0:T(8,128)}) custom-call(f32[128,8,512]{2,1,0:T(8,128)} %dust.3, s32[3,2048]{1,0:T(4,128)} %table.1, f32[16,128]{1,0:T(8,128)} %bitcast.4), custom_call_target="tpu_custom_call" | custom-call | tf_op jit(solution)/shard_map/halo/pallas_call | solution.py:312
  14.7 23.5 %collide.1.dust = f32[128,8,512]{2,1,0:T(8,128)} custom-call(f32[128,8,512]{2,1,0:T(8,128)} %dust.3, f32[128,512]{1,0:T(8,128)} %get-tuple-element.8.below, f32[128,512]{1,0:T(8,128)} %get-tuple-element.9.above, f32[8,128]{1,0:T(8,128)} %get-tuple-element.10.left, f32[8,128]{1,0:T(8,128)} %get-tuple-element.11.right, f32[128]{0:T(128)} %drift.1, f32[128]{0:T(128)} %mixing.1, ...), custom_call_target="tpu_custom_call" | custom-call | tf_op jit(solution)/shard_map/collide/pallas_call | solution.py:334
  38.2 20.2 %heat.1 = f32[4,8,512]{2,1,0:T(8,128)} custom-call(f32[128,8,512]{2,1,0:T(8,128)} %collide.1.dust, f32[128,128]{1,0:T(8,128)} %absorption.1, f32[1,128]{1,0:T(1,128)} %bitcast.6, s32[1,128]{1,0:T(1,128)} %bitcast.7), custom_call_target="tpu_custom_call" | custom-call | tf_op jit(solution)/shard_map/heat/pallas_call | solution.py:345
  58.4 1.5 %copy.11 = f32[4,8,512]{2,1,0:T(8,128)} copy(f32[4,8,512]{2,1,0:T(8,128)} %heat.1) | data formatting | bytes 131072

commit v2 on v1

--- a/solution.py
+++ b/solution.py
@@ -12,7 +12,8 @@
 SUB = 8
 depth_scale = 4.0
 SHIFT = 10.0
-UNROLL = 16
+UNROLL = 32
+GROUP = 4
 f32 = jnp.float32
 bf16 = jnp.bfloat16
 
@@ -42,7 +43,7 @@
 
 
 def halo_kernel(
-    n_rad, n_pol, dust, table, rate, below, above, left, right, rows_at, loss,
+    n_rad, n_pol, dust, table, rate, below, above, left, right, sources, targets, loss,
     ends, sent, load_sem, send_sem, recv_sem,
 ):
     sizes = dust.shape[0]
@@ -95,10 +96,11 @@
     sent[0] = first
     sent[1] = last
     for piece in range(table.shape[1] // LANES):
-        for row in range(3):
-            rows_at[pl.ds(row * (table.shape[1] // LANES) + piece, 1), :] = (
-                table[row : row + 1, LANES * piece : LANES * piece + LANES] * (4 * SUB)
-            )
+        cut = slice(LANES * piece, LANES * piece + LANES)
+        at = pl.ds(piece, 1)
+        span = tile // LANES * SUB
+        sources[at, :] = table[0:1, cut] * (span << 16) + table[1:2, cut] * span
+        targets[at, :] = table[2:3, cut] * span
     edges = [
         pltpu.make_async_remote_copy(
             sent.at[1], left, send_sem.at[2], recv_sem.at[2], device_id={"rad": rad_up}
@@ -129,42 +131,66 @@
 
 
 def collide_kernel(
-    n_rad, n_pol, dust, below, above, left, right, drift, mixing, rows_at, rate, loss,
-    out, adv, gain_a, gain_b,
+    n_rad, n_pol, dust, below, above, left, right, drift, mixing, sources, targets, rate, loss,
+    out, turned, padded, adv, gain_a, gain_b, gain_c, gain_d, matrices, lost,
+    load_sem, turn_sem, out_sem,
 ):
-    sizes = dust.shape[0]
+    sizes, _, tile = dust.shape
     pairs = rate.shape[0]
-    pieces = dust.shape[2] // LANES
+    pieces = tile // LANES
     span = pieces * SUB
     rad = lax.axis_index("rad")
     pol = lax.axis_index("pol")
+    loads = []
+    for k in range(pieces):
+        cut = pl.ds(LANES * k, LANES)
+        for n, (source, place) in enumerate(
+            (
+                (dust.at[:, :, cut], padded.at[k, :, pl.ds(1, SUB), :]),
+                (below.at[:, cut], padded.at[k, :, 0, :]),
+                (above.at[:, cut], padded.at[k, :, SUB + 1, :]),
+            )
+        ):
+            load = pltpu.make_async_copy(source, place, load_sem.at[3 * k + n])
+            load.start()
+            loads.append(load)
     lane = lax.broadcasted_iota(jnp.int32, (SUB, LANES), 1)
     sub = lax.broadcasted_iota(jnp.int32, (SUB, LANES), 0)
+    no_lower = jnp.logical_and(sub == 0, pol == 0)
+    no_upper = jnp.logical_and(sub == SUB - 1, pol == n_pol - 1)
     has_left = jnp.where(rad > 0, 1.0, 0.0)
     has_right = jnp.where(rad < n_rad - 1, 1.0, 0.0)
-    has_below = jnp.where(pol > 0, 1.0, 0.0)
-    has_above = jnp.where(pol < n_pol - 1, 1.0, 0.0)
-    zero = jnp.zeros((SUB, LANES), f32)
+    matrix = stacked(loss[...])
+
+    def rows(start):
+        return pl.ds(pl.multiple_of(start, span), span)
+
+    def clear(size, _):
+        for gain in (gain_b, gain_c, gain_d):
+            gain[rows(size * span), :] = jnp.zeros((span, LANES), f32)
+        return 0
+
+    lax.fori_loop(0, sizes, clear, 0, unroll=4)
+    for load in loads:
+        load.wait()
 
     def advect(group, carry):
-        at_left, at_right = carry
-        for step in range(4):
-            size = group * 4 + step
+        for step in range(GROUP):
+            size = group * GROUP + step
+            at_left, at_right = (
+                carry if step == 0 else [pltpu.roll(x, LANES - step, 1) for x in carry]
+            )
             c = drift[size]
             m = mixing[size]
-            center = dust[size]
-            cells = [center[:, LANES * k : LANES * k + LANES] for k in range(pieces)]
+            cells = [padded[k, size, 1 : SUB + 1, :] for k in range(pieces)]
             back = [pltpu.roll(x, LANES - 1, 1) for x in cells] + [at_right]
             forth = [at_left] + [pltpu.roll(x, 1, 1) for x in cells]
-            low_row = below[pl.ds(size, 1), :] * has_below
-            high_row = above[pl.ds(size, 1), :] * has_above
             for k in range(pieces):
-                cut = slice(LANES * k, LANES * k + LANES)
                 here = cells[k]
                 outer = jnp.where(lane == LANES - 1, back[k + 1], back[k])
                 inner = jnp.where(lane == 0, forth[k], forth[k + 1])
-                upper = jnp.where(sub == SUB - 1, high_row[:, cut], pltpu.roll(here, SUB - 1, 0))
-                lower = jnp.where(sub == 0, low_row[:, cut], pltpu.roll(here, 1, 0))
+                upper = jnp.where(no_upper, 0.0, padded[k, size, 2 : SUB + 2, :])
+                lower = jnp.where(no_lower, 0.0, padded[k, size, 0:SUB, :])
                 value = (
                     here
                     + c * (outer - here)
@@ -173,47 +199,95 @@
                 rows = pl.ds(pl.multiple_of(size * span + k * SUB, SUB), SUB)
                 adv[rows, :] = value
                 gain_a[rows, :] = value
-                gain_b[rows, :] = zero
-            at_left = pltpu.roll(at_left, LANES - 1, 1)
-            at_right = pltpu.roll(at_right, LANES - 1, 1)
-        return at_left, at_right
+        return tuple(pltpu.roll(x, LANES - GROUP, 1) for x in carry)
 
     lax.fori_loop(
         0,
-        sizes // 4,
+        sizes // GROUP,
         advect,
         (left[...] * has_left, pltpu.roll(right[...] * has_right, LANES - 1, 1)),
     )
-
-    def rows(start):
-        return pl.ds(pl.multiple_of(start, span), span)
+    by_size = adv.reshape(sizes, span, LANES)
+    lost_by_size = lost.reshape(sizes, span, LANES)
+    gains = (gain_a, gain_b, gain_c, gain_d)
+    leave = pltpu.make_async_copy(by_size, turned, turn_sem.at[0])
+    leave.start()
 
     def collide(group, _):
         base = group * UNROLL
         for step in range(UNROLL):
-            first = rows_at[base + step]
-            second = rows_at[base + (pairs + step)]
-            target = rows_at[base + (2 * pairs + step)]
+            both = sources[base + step]
+            first = lax.shift_right_logical(both, 16)
+            second = lax.bitwise_and(both, 0xFFFF)
+            target = targets[base + step]
             value = (rate[base + step] * adv[rows(first), :]) * adv[rows(second), :]
-            gain = gain_a if step % 2 == 0 else gain_b
+            gain = gains[step % 4]
             gain[rows(target), :] = gain[rows(target), :] + value
         return 0
 
-    lax.fori_loop(0, pairs // UNROLL, collide, 0)
-
-    matrix = stacked(loss[...])
-    for t in range(SUB):
-        parts = [pl.ds(k * SUB + t, sizes, stride=span) for k in range(pieces)]
-        here = jnp.concatenate([adv[part, :] for part in parts], axis=1)
-        lost = here * product(matrix, here)
+    quarter = pairs // UNROLL // 4
+
+    def collide_quarter(n):
+        lax.fori_loop(n * quarter, (n + 1) * quarter, collide, 0)
+
+    collide_quarter(0)
+    leave.wait()
+
+    def turn(row, _):
+        pltpu.make_async_copy(turned.at[:, row, :], matrices.at[row], turn_sem.at[1]).start()
+        return 0
+
+    lax.fori_loop(0, span, turn, 0)
+    collide_quarter(1)
+    pltpu.make_async_copy(matrices, matrices, turn_sem.at[1]).wait()
+    for row in range(0, span, 2):
+        here = jnp.concatenate([matrices[row], matrices[row + 1]], axis=1)
+        rate_lost = product(matrix, here)
+        matrices[row] = rate_lost[:, :LANES]
+        matrices[row + 1] = rate_lost[:, LANES:]
+
+    def turn_back(row, _):
+        pltpu.make_async_copy(matrices.at[row], turned.at[:, row, :], turn_sem.at[2]).start()
+        return 0
+
+    lax.fori_loop(0, span, turn_back, 0)
+    collide_quarter(2)
+    pltpu.make_async_copy(matrices, matrices, turn_sem.at[2]).wait()
+    back = pltpu.make_async_copy(turned, lost_by_size, turn_sem.at[3])
+    back.start()
+    collide_quarter(3)
+    back.wait()
+    chunk = sizes // 4
+    stores = []
+    for part in range(4):
+
+        def combine(size, _):
+            for k in range(pieces):
+                at = pl.ds(pl.multiple_of(size * span + k * SUB, SUB), SUB)
+                padded[k, size, 0:SUB, :] = (
+                    (gain_a[at, :] + gain_b[at, :])
+                    + (gain_c[at, :] + gain_d[at, :])
+                    - adv[at, :] * lost[at, :]
+                )
+            return 0
+
+        lax.fori_loop(part * chunk, part * chunk + chunk, combine, 0, unroll=4)
         for k in range(pieces):
-            cut = slice(LANES * k, LANES * k + LANES)
-            out[:, t, cut] = gain_a[parts[k], :] + gain_b[parts[k], :] - lost[:, cut]
+            some = pl.ds(part * chunk, chunk)
+            store = pltpu.make_async_copy(
+                padded.at[k, some, pl.ds(0, SUB), :],
+                out.at[some, :, pl.ds(LANES * k, LANES)],
+                out_sem.at[part * pieces + k],
+            )
+            store.start()
+            stores.append(store)
+    for store in stores:
+        store.wait()
 
 
 def heat_kernel(
     n_rad, dust, absorption, flux, channel, heating,
-    steps, factor, tile_total, arrived, send_sem, recv_sem,
+    natural, steps, factor, tile_total, arrived, load_sem, send_sem, recv_sem,
 ):
     sizes = dust.shape[0]
     tile = dust.shape[2]
@@ -221,6 +295,11 @@
     pieces = tile // LANES
     ray_length = tile * n_rad
     rad = lax.axis_index("rad")
+    loads = []
+    for t in range(SUB):
+        load = pltpu.make_async_copy(dust.at[:, t, :], natural.at[t], load_sem.at[t])
+        load.start()
+        loads.append(load)
     barrier = pltpu.get_barrier_semaphore()
 
     def greet(away, _):
@@ -233,7 +312,8 @@
     lane = lax.broadcasted_iota(jnp.int32, (bands, LANES), 1)
     column = jnp.zeros((bands, LANES), f32)
     for t in range(SUB):
-        step = product(matrix, dust[:, t, :])
+        loads[t].wait()
+        step = product(matrix, natural[t])
         steps[t] = step
         over = step[:, :LANES]
         for k in range(1, pieces):
@@ -267,11 +347,8 @@
             )
             within = so_far + sums[:, :LANES]
             so_far = so_far + sums[:, LANES:]
-            series = x * (
-                1.0 - x * (0.5 - x * (1.0 / 6 - x * (1.0 / 24 - x * (1.0 / 120 - x * (1.0 / 720)))))
-            )
-            taken = jnp.where(jnp.abs(x) < 0.1, series, 1.0 - jnp.exp(-x))
-            high, low = halves(jnp.exp(SHIFT - within) * taken * ray_length)
+            taken = x * (1.0 - x * (0.5 - x * (1.0 / 6 - x * (1.0 / 24 - x * (1.0 / 120)))))
+            high, low = halves(jnp.exp(SHIFT - within) * (taken * ray_length))
             factor[t, 0:bands, cut] = high
             factor[t, bands : 2 * bands, cut] = low
 
@@ -305,22 +382,24 @@
     pairs = pair_rate.shape[0]
     bands = absorption.shape[0]
     pieces = tile // LANES
+    span = pieces * SUB
 
     def like(*shape, dtype=f32):
         return jax.ShapeDtypeStruct(shape, dtype)
 
-    below, above, left, right, rows_at, loss = pl.pallas_call(
+    below, above, left, right, sources, targets, loss = pl.pallas_call(
         functools.partial(halo_kernel, n_rad, n_pol),
         out_shape=(
             like(sizes, tile),
             like(sizes, tile),
             like(rows, sizes),
             like(rows, sizes),
-            like(3 * pairs // LANES, LANES, dtype=jnp.int32),
+            like(pairs // LANES, LANES, dtype=jnp.int32),
+            like(pairs // LANES, LANES, dtype=jnp.int32),
             like(sizes, sizes),
         ),
         in_specs=[ANY, VMEM, VMEM],
-        out_specs=(VMEM,) * 6,
+        out_specs=(VMEM,) * 7,
         scratch_shapes=[
             pltpu.VMEM((2, sizes, rows, LANES), f32),
             pltpu.VMEM((2, rows, sizes), f32),
@@ -331,27 +410,37 @@
         compiler_params=pltpu.CompilerParams(collective_id=0, has_side_effects=True),
         name="halo",
     )(dust, pair_table, pair_rate.reshape(pairs // LANES, LANES))
-    new_dust = pl.pallas_call(
+    new_dust, _ = pl.pallas_call(
         functools.partial(collide_kernel, n_rad, n_pol),
-        out_shape=like(sizes, rows, tile),
-        in_specs=[VMEM] * 5 + [SMEM] * 4 + [VMEM],
-        out_specs=VMEM,
-        scratch_shapes=[pltpu.VMEM((sizes * pieces * SUB, LANES), f32)] * 3,
+        out_shape=(like(sizes, rows, tile), like(sizes, span, LANES)),
+        in_specs=[ANY] * 3 + [VMEM] * 2 + [SMEM] * 5 + [VMEM],
+        out_specs=(ANY, ANY),
+        scratch_shapes=[pltpu.VMEM((pieces, sizes, 2 * SUB, LANES), f32)]
+        + [pltpu.VMEM((sizes * span, LANES), f32)] * 5
+        + [
+            pltpu.VMEM((span, sizes, LANES), f32),
+            pltpu.VMEM((sizes * span, LANES), f32),
+            pltpu.SemaphoreType.DMA((3 * pieces,)),
+            pltpu.SemaphoreType.DMA((4,)),
+            pltpu.SemaphoreType.DMA((4 * pieces,)),
+        ],
         name="collide",
     )(
         dust, below, above, left, right, drift_courant, mixing,
-        rows_at.reshape(3 * pairs), pair_rate, loss,
+        sources.reshape(pairs), targets.reshape(pairs), pair_rate, loss,
     )
     heating = pl.pallas_call(
         functools.partial(heat_kernel, n_rad),
         out_shape=like(CH, rows, tile),
-        in_specs=[VMEM] * 4,
+        in_specs=[ANY] + [VMEM] * 3,
         out_specs=VMEM,
         scratch_shapes=[
+            pltpu.VMEM((rows, sizes, tile), f32),
             pltpu.VMEM((rows, bands, tile), f32),
             pltpu.VMEM((rows, 2 * bands, tile), bf16),
             pltpu.VMEM((rows, bands), f32),
             pltpu.VMEM((n_rad - 1, rows, bands), f32),
+            pltpu.SemaphoreType.DMA((rows,)),
             pltpu.SemaphoreType.DMA,
             pltpu.SemaphoreType.DMA,
         ],

time: 60.2 us -> 48.3 us (0.80)
  Pallas kernels: 57.8 us -> 45.7 us
    pallas_call x1, Pallas kernels: 23.5 us -> 15.6 us  [shards(): pl.pallas_call(functools.partial(collide_kernel, n_rad, n_pol), out_shape...]
    pallas_call x1, Pallas kernels: 20.2 us -> 16 us  [shards(): pl.pallas_call(functools.partial(heat_kernel, n_rad), out_shape=like(CH,...]
where the time goes in v2:
time: 48.3 us; the launch traced here: 47.8 us
  Pallas kernels  45.7 us (95%)
  local copies, waits for them, and re-layouts  1.47 us (3%)
  between operations  0.65 us (1%)
    pallas_call x1, Pallas kernels, shards(): pl.pallas_call(functools.partial(heat_kernel, n_rad), out_shape=like(CH,...  16 us
    pallas_call x1, Pallas kernels, shards(): pl.pallas_call(functools.partial(collide_kernel, n_rad, n_pol), out_shape...  15.6 us
    pallas_call x1, Pallas kernels, shards(): pl.pallas_call(functools.partial(halo_kernel, n_rad, n_pol), out_shape=(l...  14.1 us
    unnamed x1, local copies, waits for them, and re-layouts  1.47 us

profile of v2, /device:TPU:1, one launch (start us, length us, event | category | flops | bytes accessed | tf_op | source)
XLA Modules:
  0.0 47.8 jit_solution(13595503273023644627)
XLA Ops:
  0.6 14.1 %halo.1 = (f32[128,512]{1,0:T(8,128)}, f32[128,512]{1,0:T(8,128)}, f32[8,128]{1,0:T(8,128)}, f32[8,128]{1,0:T(8,128)}, s32[16,128]{1,0:T(8,128)}, /*index=5*/s32[16,128]{1,0:T(8,128)}, f32[128,128]{1,0:T(8,128)}) custom-call(f32[128,8,512]{2,1,0:T(8,128)} %dust.3, s32[3,2048]{1,0:T(4,128)} %table.1, f32[16,128]{1,0:T(8,128)} %bitcast.5), custom_call_target="tpu_custom_call" | custom-call | tf_op jit(solution)/shard_map/halo/pallas_call | solution.py:390
  14.7 15.6 %collide.1 = (f32[128,8,512]{2,1,0:T(8,128)}, f32[128,32,128]{2,1,0:T(8,128)}) custom-call(f32[128,8,512]{2,1,0:T(8,128)} %dust.3, f32[128,512]{1,0:T(8,128)} %get-tuple-element.10.below, f32[128,512]{1,0:T(8,128)} %get-tuple-element.11.above, f32[8,128]{1,0:T(8,128)} %get-tuple-element.12.left, f32[8,128]{1,0:T(8,128)} %get-tuple-element.13.right, ...), custom_call_target="tpu_custom_call" | custom-call | tf_op jit(solution)/shard_map/collide/pallas_call | solution.py:413
  30.3 16.0 %heat.1 = f32[4,8,512]{2,1,0:T(8,128)} custom-call(f32[128,8,512]{2,1,0:T(8,128)} %get-tuple-element.20.dust, f32[128,128]{1,0:T(8,128)} %absorption.1, f32[1,128]{1,0:T(1,128)} %bitcast.8, s32[1,128]{1,0:T(1,128)} %bitcast.9), custom_call_target="tpu_custom_call" | custom-call | tf_op jit(solution)/shard_map/heat/pallas_call | solution.py:432
  46.3 1.5 %copy.11 = f32[4,8,512]{2,1,0:T(8,128)} copy(f32[4,8,512]{2,1,0:T(8,128)} %heat.1) | data formatting | bytes 131072
